TPU v7x, 32 devices: a whole 2x2x4 slice. The times are simulated.
32 devices in a mesh: grp: 4 (over z), mem: 8 (over y, x, core).
Axes of the slice: x: 2, y: 2, z: 4, core: 2. Of those that a mesh axis runs over, the one named last changes fastest.
Arguments:
- basis: float32 [20, 2048, 128], P(None, ('grp', 'mem'))
- precond: bfloat16 [2048, 128, 128], P(('grp', 'mem'))
- leaf_rows: float32 [1024, 128], P(('grp', 'mem')), may hold values from -6 to 6
- leaf_fiber: int32 [1024], P(('grp', 'mem')), may hold values from 0 to 63
- strad_rows: float32 [1024, 128], P(('grp', 'mem')), may hold values from -6 to 6
- strad_fiber: int32 [1024], P(('grp', 'mem')), may hold values from 0 to 63
- strad_count: int32 [32, 4], P(('grp', 'mem')), may hold values from 0 to 8, as said below
Outputs:
- coeffs: float32 [21], replicated
- next_vector: float32 [2048, 128], P(('grp', 'mem'))
Inputs may be any that keep to these rules, and one draw needn't show every extreme that they name: `leaf_fiber`: a destination fiber within the destination device. `strad_fiber`: a fiber of the receiving device. The first strad_count slots of a block are live, the rest are not read; some device fills a block.
All inputs are finite; a program needn't handle non-finite values.
Results may differ from a plain program's by a relative error of at most 0.0011.
Values sent between devices are 32-bit elements; how exact they have to be, the bound alone decides.
A program may use at most 64 MiB of HBM per device.

v0:
```python
import jax
import jax.numpy as jnp
from jax import lax
from jax.sharding import PartitionSpec as P

EPS = 1e-06


def local(basis, precond, leaf_rows, leaf_fiber, strad_rows, strad_fiber, strad_count):
    groups = lax.axis_size("grp")
    members = lax.axis_size("mem")
    krylov, fibers_here, width = basis.shape
    fiber_index = jnp.arange(fibers_here, dtype=jnp.int32)
    arrived, arrived_ids = (
        lax.all_to_all(leaf_rows, "mem", split_axis=0, concat_axis=0, tiled=True),
        lax.all_to_all(
            leaf_fiber.astype(jnp.float32), "mem", split_axis=0, concat_axis=0, tiled=True
        ),
    )
    select = (fiber_index[:, None] == arrived_ids.astype(jnp.int32)[None, :]).astype(jnp.float32)
    far_field = jnp.dot(
        select, arrived, precision=lax.Precision.HIGHEST, preferred_element_type=jnp.float32
    )
    strad_slots = strad_rows.shape[0] // groups
    keeping = (jnp.arange(strad_slots, dtype=jnp.int32)[None, :] < strad_count[0][:, None]).reshape(
        -1
    )
    outgoing = strad_rows * keeping[:, None].astype(jnp.float32)
    incoming = lax.all_to_all(outgoing, "grp", split_axis=0, concat_axis=0, tiled=True)
    select_near = (fiber_index[:, None] == strad_fiber[None, :]).astype(jnp.float32)
    near_field = jnp.dot(
        select_near, incoming, precision=lax.Precision.HIGHEST, preferred_element_type=jnp.float32
    )
    field = (basis[krylov - 1] + far_field + near_field).astype(jnp.bfloat16)
    applied = jnp.einsum("fij,fj->fi", precond, field, preferred_element_type=jnp.float32)
    total = float(fibers_here * width * groups * members)
    local_coef = jnp.einsum("kfi,fi->k", basis, applied, precision=lax.Precision.HIGHEST)
    gram_local = jnp.einsum("kfi,lfi->kl", basis, basis, precision=lax.Precision.HIGHEST)
    coef_sum, square_sum, gram_sum = lax.psum(
        (local_coef, jnp.sum(applied * applied), gram_local), ("grp", "mem")
    )
    coef = coef_sum / total
    gram = gram_sum / total
    residual = applied - jnp.einsum("k,kfi->fi", coef, basis, precision=lax.Precision.HIGHEST)
    projected = jnp.dot(gram, coef, precision=lax.Precision.HIGHEST)
    square = square_sum / total - 2.0 * jnp.sum(coef * coef) + jnp.sum(coef * projected)
    beta = jnp.sqrt(square + EPS)
    return (jnp.concatenate([coef, beta[None]]), residual / beta)


def solution(mesh):
    return jax.shard_map(
        local,
        mesh=mesh,
        in_specs=(
            P(None, ("grp", "mem"), None),
            P(("grp", "mem"), None, None),
            P(("grp", "mem"), None),
            P(("grp", "mem")),
            P(("grp", "mem"), None),
            P(("grp", "mem")),
            P(("grp", "mem"), None),
        ),
        out_specs=(P(), P(("grp", "mem"), None)),
        check_vma=False,
    )
```

profile of v0, /device:TPU:0, one launch (start us, length us, event | category | flops | bytes accessed | tf_op | source)
XLA Modules:
  0.0 79.5 jit_solution(3475346898591158441)
XLA Ops:
  0.6 0.0 copy-start
  0.7 0.8 %convert_element_type.29 = f32[32]{0:T(128)S(1)} convert(s32[32]{0:T(128)} %param.10) | non-fusion elementwise | flops 32 | bytes 256 | tf_op jit(solution)/shard_map/convert_element_type | solution.py:17
  1.5 0.7 all_to_all.22
  2.1 5.2 %all-to-all-start = ((f32[8,4,1]{1,2,0:T(1,128)}), f32[8,4,1]{1,2,0:T(1,128)S(1)}, u32[]{:S(2)}, u32[]{:S(2)}) async-start(f32[8,4,1]{1,2,0:T(1,128)} %bitcast.1), calls=%async_computation | async-start | bytes 8192 | tf_op jit(solution)/shard_map/all_to_all | solution.py:16
  7.3 0.7 fusion.16
  8.1 0.1 reshape.35
  8.2 1.4 %multiply_bitcast_fusion = f32[4,8,128]{2,1,0:T(8,128)} fusion(f32[32,128]{1,0:T(8,128)} %param.11, f32[32]{0:T(128)S(1)} %reshape.35), kind=kLoop, calls=%fused_computation.21 | loop fusion | flops 4096 | bytes 32896 | tf_op jit(solution)/shard_map/all_to_all | solution.py:29
  9.5 2.8 %convolution_bitcast_fusion = f32[20,20]{1,0:T(8,128)S(1)} fusion(f32[20,64,128]{2,1,0:T(8,128)} %param.7), kind=kOutput, calls=%fused_computation.4 | convolution fusion | flops 39321600 | bytes 656960 | tf_op jit(solution)/shard_map/kfi,lfi->kl/dot_general | solution.py:38
  12.3 4.2 %all-to-all-start.1 = ((f32[8,4,128]{2,1,0:T(4,128)}), f32[8,4,128]{2,1,0:T(4,128)S(1)}, u32[]{:S(2)}, u32[]{:S(2)}) async-start(f32[8,4,128]{2,1,0:T(4,128)} %bitcast.45), calls=%async_computation.1 | async-start | bytes 32768 | tf_op jit(solution)/shard_map/all_to_all | solution.py:15
  16.5 0.1 convert_element_type.31
  16.6 4.7 %all-to-all-done.1 = f32[8,4,128]{2,1,0:T(4,128)S(1)} async-done(((f32[8,4,128]{2,1,0:T(4,128)}), f32[8,4,128]{2,1,0:T(4,128)S(1)}, u32[]{:S(2)}, u32[]{:S(2)}) %all-to-all-start.1) | async-done | bytes 16416 | tf_op jit(solution)/shard_map/all_to_all | solution.py:15
  21.3 4.9 %all-to-all-start.2 = ((f32[4,8,128]{2,1,0:T(8,128)}), f32[4,8,128]{2,1,0:T(8,128)S(1)}, u32[]{:S(2)}, u32[]{:S(2)}) async-start(f32[4,8,128]{2,1,0:T(8,128)} %multiply_bitcast_fusion), calls=%async_computation.2 | async-start | bytes 32768 | tf_op jit(solution)/shard_map/all_to_all | solution.py:29
  26.2 0.9 %convolution_add_fusion.1 = f32[64,128]{1,0:T(8,128)S(1)} fusion(f32[32,128]{1,0:T(8,128)S(1)} %bitcast.44, f32[20,64,128]{2,1,0:T(8,128)} %param.7, s32[32]{0:T(128)S(1)} %convert_element_type.31), kind=kOutput, calls=%fused_computation.1 | convolution fusion | flops 3155968 | bytes 82048 | tf_op jit(solution)/shard_map/dot_general | solution.py:21
  27.1 4.7 %all-to-all-done.2 = f32[4,8,128]{2,1,0:T(8,128)S(1)} async-done(((f32[4,8,128]{2,1,0:T(8,128)}), f32[4,8,128]{2,1,0:T(8,128)S(1)}, u32[]{:S(2)}, u32[]{:S(2)}) %all-to-all-start.2) | async-done | bytes 16416 | tf_op jit(solution)/shard_map/all_to_all | solution.py:29
  31.8 0.8 %fusion.1 = bf16[64,128,1]{1,0,2:T(8,128)(2,1)S(1)} fusion(f32[64,128]{1,0:T(8,128)S(1)} %convolution_add_fusion.1, f32[4,8,128]{2,1,0:T(8,128)S(1)} %all-to-all-done.2, s32[32]{0:T(128)} %param.12), kind=kOutput, calls=%fused_computation.3 | convolution fusion | flops 3164160 | bytes 65664 | tf_op jit(solution)/shard_map/dot_general | solution.py:31
  32.6 1.2 %fusion.9 = f32[64,1,128]{2,1,0:T(1,128)S(1)} fusion(bf16[64,128,128]{2,1,0:T(8,128)(2,1)S(1)} %copy-done, bf16[64,128,1]{1,0,2:T(8,128)(2,1)S(1)} %fusion.1), kind=kOutput, calls=%fused_computation.14 | convolution fusion | flops 2097152 | bytes 2146304 | tf_op jit(solution)/shard_map/fij,fj->fi/dot_general | solution.py:35
  33.8 1.1 %convolution_bitcast_fusion.2 = f32[20]{0:T(128)S(1)} fusion(f32[20,64,128]{2,1,0:T(8,128)S(1)} %copy-done.1, f32[64,1,128]{2,1,0:T(1,128)S(1)} %fusion.9), kind=kOutput, calls=%fused_computation.7 | convolution fusion | flops 1966080 | bytes 688208 | tf_op jit(solution)/shard_map/kfi,fi->k/dot_general | solution.py:37
  34.8 0.6 multiply_reduce_fusion
  35.5 38.5 %all-reduce = (f32[]{:T(128)}, f32[20]{0:T(128)S(1)}, f32[20,20]{1,0:T(8,128)S(1)}) all-reduce(f32[]{:T(128)} %multiply_reduce_fusion, f32[20]{0:T(128)S(1)} %convolution_bitcast_fusion.2, f32[20,20]{1,0:T(8,128)S(1)} %convolution_bitcast_fusion), channel_id=1, replica_groups=mesh['grp'=4,'mem'=8] {'grp','mem'}, use_global_device_ids=true, to_apply=%region_2.0 | all-reduce | flops 421 | bytes 3368 | tf_op jit(solution)/shard_map/psum | solution.py:39
  74.0 0.6 broadcast_multiply_fusion
  74.6 0.9 %fusion.3 = f32[1,64,128]{2,0,1:T(1,128)S(1)} fusion(f32[20,64,128]{2,1,0:T(8,128)S(1)} %copy-done.1, f32[20]{0:T(128)S(1)} %get-tuple-element.3), kind=kOutput, calls=%fused_computation.8 | convolution fusion | flops 1966100 | bytes 688208 | tf_op jit(solution)/shard_map/k,kfi->fi/dot_general | solution.py:44
  75.5 0.8 %fusion.7 = f32[]{:T(128)} fusion(f32[20,20]{1,0:T(8,128)S(1)} %get-tuple-element.4, f32[20]{0:T(128)S(1)} %get-tuple-element.3), kind=kOutput, calls=%fused_computation.12 | convolution fusion | flops 5279 | bytes 1684 | tf_op jit(solution)/shard_map/dot_general | solution.py:45
  78.3 0.6 subtract_divide_fusion
  78.9 0.6 pad_maximum_fusion
  (5 shorter events, 0.0 us)
Async XLA Ops:
  0.6 31.9 %copy-start = (bf16[64,128,128]{2,1,0:T(8,128)(2,1)S(1)}, bf16[64,128,128]{2,1,0:T(8,128)(2,1)}, u32[]{:S(2)}) copy-start(bf16[64,128,128]{2,1,0:T(8,128)(2,1)} %param.8) | copy-start | bytes 6291460
  0.6 33.1 %copy-start.1 = (f32[20,64,128]{2,1,0:T(8,128)S(1)}, f32[20,64,128]{2,1,0:T(8,128)}, u32[]{:S(2)}) copy-start(f32[20,64,128]{2,1,0:T(8,128)} %param.7) | copy-start | bytes 1966084
  2.1 10.2 %all-to-all-start = ((f32[8,4,1]{1,2,0:T(1,128)}), f32[8,4,1]{1,2,0:T(1,128)S(1)}, u32[]{:S(2)}, u32[]{:S(2)}) async-start(f32[8,4,1]{1,2,0:T(1,128)} %bitcast.1), calls=%async_computation | async-start | bytes 8192 | tf_op jit(solution)/shard_map/all_to_all | solution.py:16
  12.3 9.0 %all-to-all-start.1 = ((f32[8,4,128]{2,1,0:T(4,128)}), f32[8,4,128]{2,1,0:T(4,128)S(1)}, u32[]{:S(2)}, u32[]{:S(2)}) async-start(f32[8,4,128]{2,1,0:T(4,128)} %bitcast.45), calls=%async_computation.1 | async-start | bytes 32768 | tf_op jit(solution)/shard_map/all_to_all | solution.py:15
  21.3 10.5 %all-to-all-start.2 = ((f32[4,8,128]{2,1,0:T(8,128)}), f32[4,8,128]{2,1,0:T(8,128)S(1)}, u32[]{:S(2)}, u32[]{:S(2)}) async-start(f32[4,8,128]{2,1,0:T(8,128)} %multiply_bitcast_fusion), calls=%async_computation.2 | async-start | bytes 32768 | tf_op jit(solution)/shard_map/all_to_all | solution.py:29
where the time goes:
time: 80.1 us; the launch traced here: 79.5 us
  blocking collectives  38.5 us (48%)
  starting transfers between devices  14.3 us (18%)
  waiting for transfers between devices  9.37 us (12%)
  matrix products  8.4 us (10%)
  other arithmetic  5.37 us (7%)
  between operations  2.73 us (3%)
  local copies, waits for them, and re-layouts  0.86 us (1%)
    psum x1, blocking collectives, local(): lax.psum((local_coef, jnp.sum(applied * applied), gram_local), ('grp', 'm...  38.5 us
    all_to_all x1, starting transfers between devices, local(): lax.all_to_all(leaf_fiber.astype(jnp.float32), 'mem', split_axis=0, conca...  5.2 us
    all_to_all x1, starting transfers between devices, local(): lax.all_to_all(outgoing, 'grp', split_axis=0, concat_axis=0, tiled=True)  4.88 us
    all_to_all x1, waiting for transfers between devices, local(): lax.all_to_all(outgoing, 'grp', split_axis=0, concat_axis=0, tiled=True)  4.71 us
    all_to_all x1, waiting for transfers between devices, local(): lax.all_to_all(leaf_rows, 'mem', split_axis=0, concat_axis=0, tiled=True)  4.65 us
    all_to_all x1, starting transfers between devices, local(): lax.all_to_all(leaf_rows, 'mem', split_axis=0, concat_axis=0, tiled=True)  4.21 us
    dot_general x1, matrix products, local(): jnp.einsum('kfi,lfi->kl', basis, basis, precision=lax.Precision.HIGHEST)  2.75 us
  transfers between devices with their start and end apart: 3, of which 2 were waited for; matrix products, arithmetic and copies ran while one was open for 7% of the time, Pallas kernels for 0%

commit v1 on v0

v1 whole, which is shorter than its diff:
```python
import functools

import jax
import jax.numpy as jnp
from jax import lax
from jax.experimental import pallas as pl
from jax.experimental.pallas import tpu as pltpu
from jax.sharding import PartitionSpec as P

EPS = 1e-06
MESH = pl.DeviceIdType.MESH
NT = (((1,), (1,)), ((), ()))
TN = (((0,), (0,)), ((), ()))


def iota(shape, axis):
    return lax.broadcasted_iota(jnp.int32, shape, axis)


def row_to_column(row, rows):
    shape = (rows, row.shape[1])
    diagonal = iota(shape, 0) == iota(shape, 1)
    return jnp.sum(jnp.where(diagonal, row, 0.0), axis=1, keepdims=True)


def split3(x):
    high = x.astype(jnp.bfloat16)
    rest = x - high.astype(jnp.float32)
    mid = rest.astype(jnp.bfloat16)
    low = (rest - mid.astype(jnp.float32)).astype(jnp.bfloat16)
    return high, mid, low


def kernel(
    groups, members, krylov, fibers, total,
    basis_h, precond_h, leaf_h, leaf_id_h, strad_h, strad_id_h, count_h,
    coef_ref, next_ref,
    basis, precond, leaf, leaf_id, strad, strad_id, count,
    leaf_out, leaf_in, strad_out, strad_in,
    gram_out, gram_in, gram2_out, gram2_in, dots_out, dots_in,
    field_ref, local_sem, sem,
):
    g, m = lax.axis_index("grp"), lax.axis_index("mem")
    devices = groups * members
    me = g * members + m
    width = basis.shape[1]
    cap = leaf.shape[0] // members
    slots = strad.shape[0] // groups

    barrier = pltpu.get_barrier_semaphore()
    mates = [lax.rem(m + o, members) for o in range(1, members)]
    peers = [lax.rem(g + o, groups) for o in range(1, groups)]
    for mate in mates:
        pl.semaphore_signal(barrier, inc=1, device_id=(g, mate), device_id_type=MESH)
    for peer in peers:
        pl.semaphore_signal(barrier, inc=1, device_id=(peer, m), device_id_type=MESH)

    loads = [
        pltpu.make_async_copy(src, dst, local_sem.at[i])
        for i, (src, dst) in enumerate(
            [
                (leaf_h, leaf), (leaf_id_h, leaf_id), (strad_h, strad),
                (count_h, count), (strad_id_h, strad_id),
                (basis_h, basis), (precond_h, precond),
            ]
        )
    ]
    for load in loads:
        load.start()
    for load in loads[:5]:
        load.wait()

    leaf_rows = leaf.shape[0]
    ids = jnp.broadcast_to(
        row_to_column(leaf_id[...].astype(jnp.float32), leaf_rows), (leaf_rows, width)
    )
    rows = leaf[...]
    for d in range(members):
        leaf_out[d, :cap, :] = rows[d * cap:(d + 1) * cap]
        leaf_out[d, cap:, :] = ids[d * cap:(d + 1) * cap]
    strad_rows = strad.shape[0]
    shape = (strad_rows, groups)
    of_group = iota(shape, 0) // slots == iota(shape, 1)
    live = jnp.sum(
        jnp.where(of_group, count[...].astype(jnp.float32), 0.0), axis=1, keepdims=True
    )
    within = (iota((strad_rows, 1), 0) % slots).astype(jnp.float32)
    kept = jnp.where(within < live, strad[...], 0.0)
    strad_out[...] = kept.reshape(groups, slots, width)
    leaf_in[m] = leaf_out[m]
    strad_in[g] = strad_out[g]
    strad_column = row_to_column(strad_id[...].astype(jnp.float32), strad_rows)
    fiber = iota((1, fibers), 1).astype(jnp.float32)
    strad_sel = (strad_column == fiber).astype(jnp.bfloat16)

    pl.semaphore_wait(barrier, members - 1 + groups - 1)

    def send(src, dst, pair, device):
        pltpu.make_async_remote_copy(
            src_ref=src, dst_ref=dst, send_sem=sem.at[pair], recv_sem=sem.at[pair + 1],
            device_id=device, device_id_type=MESH,
        ).start()

    def wait_bytes(ref, i):
        pltpu.make_async_copy(ref, ref, sem.at[i]).wait()

    for peer in peers[::-1]:
        send(strad_out.at[peer], strad_in.at[g], 2, (peer, m))
    for mate in mates[::-1]:
        send(leaf_out.at[mate], leaf_in.at[m], 0, (g, mate))

    loads[5].wait()
    step = 8
    tiles = pl.cdiv(krylov, 8)
    padded = tiles * 8
    lanes = 1 << (padded - 1).bit_length()

    def gram_step(c, acc):
        parts = []
        for j in range(step):
            x = basis[pl.ds(c * step + j, krylov, stride=fibers), :]
            x = jnp.concatenate(
                [x, jnp.zeros((padded - krylov, width), jnp.float32)], axis=0
            )
            parts.append(x)
        x = jnp.concatenate(parts, axis=1)
        high, mid, low = split3(x)
        stack = jnp.concatenate(
            [high.astype(jnp.float32), mid.astype(jnp.float32), low.astype(jnp.float32)], axis=0
        ).astype(jnp.bfloat16)
        return acc + lax.dot_general(stack, stack, NT, preferred_element_type=jnp.float32)

    nine = lax.fori_loop(
        0, fibers // step, gram_step, jnp.zeros((3 * padded, 3 * padded), jnp.float32)
    )
    tall = nine[:padded] + nine[padded:2 * padded] + nine[2 * padded:]
    gram = tall[:, :padded] + tall[:, padded:2 * padded] + tall[:, 2 * padded:]
    gram = jnp.concatenate(
        [gram, jnp.zeros((padded, lanes - padded), jnp.float32)], axis=1
    )
    gram_tile = jnp.concatenate(
        [gram[8 * t:8 * t + 8] for t in range(tiles)], axis=1
    )
    gram_lanes = gram_out.shape[1]
    if gram_lanes > tiles * lanes:
        gram_tile = jnp.concatenate(
            [gram_tile, jnp.zeros((8, gram_lanes - tiles * lanes), jnp.float32)], axis=1
        )
    gram_out[...] = gram_tile
    gram_in[m] = gram_tile
    loads[6].wait()
    for mate in mates[::-1]:
        send(gram_out, gram_in.at[m], 4, (g, mate))

    wait_bytes(leaf_in.at[pl.ds(0, members - 1)], 1)
    wait_bytes(strad_in.at[pl.ds(0, groups - 1)], 3)
    leaf_got = leaf_in[...]
    named = pltpu.roll(leaf_got, cap, 1).reshape(members * 2 * cap, width)[:, :fibers]
    is_row = iota((members * 2 * cap, 1), 0) % (2 * cap) < cap
    leaf_sel = ((named == fiber) & is_row).astype(jnp.float32)
    sel = jnp.concatenate([leaf_sel, strad_sel.astype(jnp.float32)], axis=0)
    got = jnp.concatenate(
        [
            leaf_got.reshape(members * 2 * cap, width),
            strad_in[...].reshape(strad_rows, width),
        ],
        axis=0,
    )
    sel = sel.astype(jnp.bfloat16)
    high, mid, low = split3(got)
    moved = (
        lax.dot_general(sel, high, TN, preferred_element_type=jnp.float32)
        + lax.dot_general(sel, mid, TN, preferred_element_type=jnp.float32)
        + lax.dot_general(sel, low, TN, preferred_element_type=jnp.float32)
    )
    field = basis[(krylov - 1) * fibers:, :] + moved
    field_ref[...] = field.astype(jnp.bfloat16).astype(jnp.float32)

    wait_bytes(gram_in.at[pl.ds(0, members - 1)], 5)
    gram_sum = jnp.sum(gram_in[...], axis=0)
    gram2_out[...] = gram_sum
    gram2_in[g] = gram_sum

    block = 16
    pieces = []
    for t in range(fibers // block):
        tile = field_ref[t * block:(t + 1) * block, :]
        lhs = jnp.concatenate(
            [
                jnp.where(iota((block, width), 0) == j, tile, 0.0).astype(jnp.bfloat16)
                for j in range(block)
            ],
            axis=1,
        )
        rhs = jnp.concatenate([precond[t * block + j] for j in range(block)], axis=1)
        pieces.append(lax.dot_general(lhs, rhs, NT, preferred_element_type=jnp.float32))
    applied = jnp.concatenate(pieces, axis=0)

    sums = []
    for k in range(krylov + 1):
        other = applied if k == krylov else basis[k * fibers:(k + 1) * fibers, :]
        product = jnp.sum((other * applied).reshape(fibers // 8, 8, width), axis=0)
        sums.append(jnp.sum(product, axis=0, keepdims=True))
    rows_of = pl.cdiv(krylov + 1, 8) * 8
    sums.append(jnp.zeros((rows_of - krylov - 1, width), jnp.float32))
    column = jnp.sum(jnp.concatenate(sums, axis=0), axis=1, keepdims=True)
    shape = (rows_of, width)
    dots = jnp.sum(
        jnp.where(iota(shape, 0) == iota(shape, 1), column, 0.0), axis=0, keepdims=True
    )
    dots_out[...] = dots
    dots_in[me] = dots
    for peer in peers[::-1]:
        send(gram2_out, gram2_in.at[g], 6, (peer, m))

    def send_dots(o, carry):
        to = lax.rem(me + devices - o, devices)
        send(dots_out, dots_in.at[me], 8, (to // members, lax.rem(to, members)))
        return carry

    lax.fori_loop(1, devices, send_dots, 0)

    wait_bytes(gram2_in.at[pl.ds(0, groups - 1)], 7)
    gram_all = jnp.sum(gram2_in[...], axis=0) / total
    wait_bytes(dots_in.at[pl.ds(0, devices - 1)], 9)
    dots = jnp.sum(dots_in[...], axis=0) / total

    lane = iota((1, width), 1)
    coef = jnp.where(lane < krylov, dots, 0.0)
    residual = applied
    for k in range(krylov):
        residual = residual - coef[:, k:k + 1] * basis[k * fibers:(k + 1) * fibers, :]
    square = jnp.sum(
        jnp.where(lane == krylov, dots, 0.0) - 2.0 * coef * coef, axis=1, keepdims=True
    )
    short = coef[:, :lanes]
    wide = jnp.concatenate([short] * (gram_lanes // lanes), axis=1)
    at = iota((8, gram_lanes), 1) // lanes
    down = jnp.zeros((8, gram_lanes), jnp.float32)
    for t in range(tiles):
        shape = (8, width)
        picked = jnp.where(iota(shape, 0) + 8 * t == iota(shape, 1), coef, 0.0)
        down = jnp.where(at == t, jnp.sum(picked, axis=1, keepdims=True), down)
    quad = jnp.sum(gram_all * down * wide, axis=0, keepdims=True)
    square = square + jnp.sum(quad, axis=1, keepdims=True)
    beta = jnp.sqrt(square + EPS)
    coef_ref[...] = jnp.where(lane == krylov, beta, coef)[:, :krylov + 1]
    next_ref[...] = residual / beta

    wait_bytes(leaf_out.at[pl.ds(0, members - 1)], 0)
    wait_bytes(strad_out.at[pl.ds(0, groups - 1)], 2)
    wait_bytes(gram_in.at[pl.ds(0, members - 1)], 4)
    wait_bytes(gram2_in.at[pl.ds(0, groups - 1)], 6)
    wait_bytes(dots_in.at[pl.ds(0, devices - 1)], 8)


def local(basis, precond, leaf_rows, leaf_fiber, strad_rows, strad_fiber, strad_count):
    groups = lax.axis_size("grp")
    members = lax.axis_size("mem")
    devices = groups * members
    krylov, fibers, width = basis.shape
    cap = leaf_rows.shape[0] // members
    slots = strad_rows.shape[0] // groups
    tiles = pl.cdiv(krylov, 8)
    lanes = 1 << (tiles * 8 - 1).bit_length()
    gram_lanes = pl.cdiv(tiles * lanes, 128) * 128
    f32, i32 = jnp.float32, jnp.int32
    any_space = pl.BlockSpec(memory_space=pl.ANY)
    vmem = pl.BlockSpec(memory_space=pltpu.VMEM)
    coeffs, vector = pl.pallas_call(
        functools.partial(
            kernel, groups, members, krylov, fibers, float(fibers * width * devices)
        ),
        out_shape=(
            jax.ShapeDtypeStruct((1, krylov + 1), f32),
            jax.ShapeDtypeStruct((fibers, width), f32),
        ),
        in_specs=[any_space] * 7,
        out_specs=(vmem, vmem),
        scratch_shapes=[
            pltpu.VMEM((krylov * fibers, width), f32),
            pltpu.VMEM(precond.shape, precond.dtype),
            pltpu.VMEM(leaf_rows.shape, f32),
            pltpu.VMEM((1, leaf_fiber.shape[0]), i32),
            pltpu.VMEM(strad_rows.shape, f32),
            pltpu.VMEM((1, strad_fiber.shape[0]), i32),
            pltpu.VMEM(strad_count.shape, i32),
            pltpu.VMEM((members, 2 * cap, width), f32),
            pltpu.VMEM((members, 2 * cap, width), f32),
            pltpu.VMEM((groups, slots, width), f32),
            pltpu.VMEM((groups, slots, width), f32),
            pltpu.VMEM((8, gram_lanes), f32),
            pltpu.VMEM((members, 8, gram_lanes), f32),
            pltpu.VMEM((8, gram_lanes), f32),
            pltpu.VMEM((groups, 8, gram_lanes), f32),
            pltpu.VMEM((1, width), f32),
            pltpu.VMEM((devices, 1, width), f32),
            pltpu.VMEM((fibers, width), f32),
            pltpu.SemaphoreType.DMA((7,)),
            pltpu.SemaphoreType.DMA((10,)),
        ],
        compiler_params=pltpu.CompilerParams(collective_id=0, has_side_effects=True),
        name="gmres_step",
    )(
        basis.reshape(krylov * fibers, width), precond, leaf_rows,
        leaf_fiber.reshape(1, -1), strad_rows, strad_fiber.reshape(1, -1), strad_count,
    )
    return coeffs.reshape(krylov + 1), vector


def solution(mesh):
    return jax.shard_map(
        local,
        mesh=mesh,
        in_specs=(
            P(None, ("grp", "mem"), None),
            P(("grp", "mem"), None, None),
            P(("grp", "mem"), None),
            P(("grp", "mem")),
            P(("grp", "mem"), None),
            P(("grp", "mem")),
            P(("grp", "mem"), None),
        ),
        out_specs=(P(), P(("grp", "mem"), None)),
        check_vma=False,
    )
```

time: 80.1 us -> 20.8 us (0.26)
  blocking collectives: 38.5 us -> 0 us
  Pallas kernels: 0 us -> 17.3 us
  starting transfers between devices: 14.3 us -> 0 us
  waiting for transfers between devices: 9.37 us -> 0 us
  matrix products: 8.4 us -> 0 us
  other arithmetic: 5.37 us -> 0 us
  between operations: 2.73 us -> 0.64 us
  local copies, waits for them, and re-layouts: 0.86 us -> 2.55 us
    psum x1 -> x0, blocking collectives: 38.5 us -> none  [local(): lax.psum((local_coef, jnp.sum(applied * applied), gram_local), ('grp', 'm...]
    pallas_call x0 -> x1, Pallas kernels: none -> 17.3 us  [local(): pl.pallas_call(functools.partial(kernel, groups, members, krylov, fibers,...]
    all_to_all x3 -> x0, starting transfers between devices: 14.3 us -> none  [the longest x1 5.2 us: local(): lax.all_to_all(leaf_fiber.astype(jnp.float32), 'mem', split_axis=0, conca...]
    all_to_all x3 -> x0, waiting for transfers between devices: 9.37 us -> none  [the longest x1 4.71 us: local(): lax.all_to_all(outgoing, 'grp', split_axis=0, concat_axis=0, tiled=True)]
    dot_general x7 -> x0, matrix products: 8.4 us -> none  [the longest x1 2.75 us: local(): jnp.einsum('kfi,lfi->kl', basis, basis, precision=lax.Precision.HIGHEST)]
    unnamed x4 -> x2, local copies, waits for them, and re-layouts: 0.02 us -> 2.55 us
    convert_element_type x3 -> x0, other arithmetic: 1.55 us -> none  [the longest x1 0.81 us: local(): leaf_fiber.astype(jnp.float32)]
    all_to_all x1 -> x0, other arithmetic: 1.39 us -> none  [local(): lax.all_to_all(outgoing, 'grp', split_axis=0, concat_axis=0, tiled=True)]
  transfers between devices with their start and end apart: 3 -> 0, of which waited for: 2 -> 0; matrix products, arithmetic and copies ran while one was open for 7% -> 0% of each run, Pallas kernels for 0% -> 0%
where the time goes in v1:
time: 20.8 us; the launch traced here: 20.5 us
  Pallas kernels  17.3 us (83%)
  local copies, waits for them, and re-layouts  2.55 us (12%)
  between operations  0.64 us (3%)
    pallas_call x1, Pallas kernels, local(): pl.pallas_call(functools.partial(kernel, groups, members, krylov, fibers,...  17.3 us
    unnamed x2, local copies, waits for them, and re-layouts  2.55 us

profile of v1, /device:TPU:0, one launch (start us, length us, event | category | flops | bytes accessed | tf_op | source)
XLA Modules:
  0.0 20.5 jit_solution(14279782874356570758)
XLA Ops:
  0.6 17.3 %gmres_step.1 = (f32[1,21]{1,0:T(1,128)}, f32[64,128]{1,0:T(8,128)}) custom-call(f32[1280,128]{1,0:T(8,128)} %bitcast.4, bf16[64,128,128]{2,1,0:T(8,128)(2,1)} %precond_h.1, f32[32,128]{1,0:T(8,128)} %leaf_h.1, s32[1,32]{1,0:T(1,128)} %bitcast.5, f32[32,128]{1,0:T(8,128)} %strad_h.1, s32[1,32]{1,0:T(1,128)} %bitcast.6, s32[1,4]{1,0:T(1,128)} %count_h.1), custom_call_target="tpu_custom_call" | custom-call | tf_op jit(solution)/shard_map/gmres_step/pallas_call | solution.py:270
  18.0 1.2 %copy.11 = f32[21]{0:T(128)} copy(f32[21]{0:T(128)} %bitcast.7) | data formatting | bytes 168
  19.1 1.4 %copy.12 = f32[64,128]{1,0:T(8,128)} copy(f32[64,128]{1,0:T(8,128)} %get-tuple-element.9) | data formatting | bytes 65536

commit v2 on v1

--- a/solution.py
+++ b/solution.py
@@ -176,11 +176,6 @@
     field = basis[(krylov - 1) * fibers:, :] + moved
     field_ref[...] = field.astype(jnp.bfloat16).astype(jnp.float32)
 
-    wait_bytes(gram_in.at[pl.ds(0, members - 1)], 5)
-    gram_sum = jnp.sum(gram_in[...], axis=0)
-    gram2_out[...] = gram_sum
-    gram2_in[g] = gram_sum
-
     block = 16
     pieces = []
     for t in range(fibers // block):
@@ -210,15 +205,25 @@
     )
     dots_out[...] = dots
     dots_in[me] = dots
+    if devices <= 64:
+        for i in range(groups * members - 1, 0, -1):
+            to = (([g] + peers)[i // members], ([m] + mates)[i % members])
+            send(dots_out, dots_in.at[me], 8, to)
+    else:
+
+        def send_dots(o, carry):
+            to = lax.rem(me + devices - o, devices)
+            send(dots_out, dots_in.at[me], 8, (to // members, lax.rem(to, members)))
+            return carry
+
+        lax.fori_loop(1, devices, send_dots, 0)
+
+    wait_bytes(gram_in.at[pl.ds(0, members - 1)], 5)
+    gram_sum = jnp.sum(gram_in[...], axis=0)
+    gram2_out[...] = gram_sum
+    gram2_in[g] = gram_sum
     for peer in peers[::-1]:
         send(gram2_out, gram2_in.at[g], 6, (peer, m))
-
-    def send_dots(o, carry):
-        to = lax.rem(me + devices - o, devices)
-        send(dots_out, dots_in.at[me], 8, (to // members, lax.rem(to, members)))
-        return carry
-
-    lax.fori_loop(1, devices, send_dots, 0)
 
     wait_bytes(gram2_in.at[pl.ds(0, groups - 1)], 7)
     gram_all = jnp.sum(gram2_in[...], axis=0) / total
@@ -252,6 +257,15 @@
     wait_bytes(gram_in.at[pl.ds(0, members - 1)], 4)
     wait_bytes(gram2_in.at[pl.ds(0, groups - 1)], 6)
     wait_bytes(dots_in.at[pl.ds(0, devices - 1)], 8)
+
+
+def put_out(coef_ref, next_ref, coef_h, next_h, sem):
+    second = pltpu.make_async_copy(next_ref, next_h, sem.at[1])
+    first = pltpu.make_async_copy(coef_ref, coef_h, sem.at[0])
+    second.start()
+    first.start()
+    first.wait()
+    second.wait()
 
 
 def local(basis, precond, leaf_rows, leaf_fiber, strad_rows, strad_fiber, strad_count):
@@ -272,8 +286,8 @@
             kernel, groups, members, krylov, fibers, float(fibers * width * devices)
         ),
         out_shape=(
-            jax.ShapeDtypeStruct((1, krylov + 1), f32),
-            jax.ShapeDtypeStruct((fibers, width), f32),
+            pltpu.VMEM((1, krylov + 1), f32),
+            pltpu.VMEM((fibers, width), f32),
         ),
         in_specs=[any_space] * 7,
         out_specs=(vmem, vmem),
@@ -305,6 +319,18 @@
         basis.reshape(krylov * fibers, width), precond, leaf_rows,
         leaf_fiber.reshape(1, -1), strad_rows, strad_fiber.reshape(1, -1), strad_count,
     )
+    coeffs, vector = pl.pallas_call(
+        put_out,
+        out_shape=(
+            jax.ShapeDtypeStruct((1, krylov + 1), f32),
+            jax.ShapeDtypeStruct((fibers, width), f32),
+        ),
+        in_specs=[vmem, vmem],
+        out_specs=(any_space, any_space),
+        scratch_shapes=[pltpu.SemaphoreType.DMA((2,))],
+        compiler_params=pltpu.CompilerParams(vmem_limit_bytes=1 << 20),
+        name="put_out",
+    )(coeffs, vector)
     return coeffs.reshape(krylov + 1), vector
 
 

time: 20.8 us -> 17 us (0.82)
  local copies, waits for them, and re-layouts: 2.55 us -> 0 us
  Pallas kernels: 17.3 us -> 16.1 us
    unnamed x2 -> x0, local copies, waits for them, and re-layouts: 2.55 us -> none
    pallas_call x1, Pallas kernels: 17.3 us -> 15.4 us  [local(): pl.pallas_call(functools.partial(kernel, groups, members, krylov, fibers,...]
    pallas_call x0 -> x1, Pallas kernels: none -> 0.63 us  [local(): pl.pallas_call(put_out, out_shape=(jax.ShapeDtypeStruct((1, krylov + 1),...]
where the time goes in v2:
time: 17 us; the launch traced here: 16.7 us
  Pallas kernels  16.1 us (95%)
  between operations  0.64 us (4%)
    pallas_call x1, Pallas kernels, local(): pl.pallas_call(functools.partial(kernel, groups, members, krylov, fibers,...  15.4 us
    pallas_call x1, Pallas kernels, local(): pl.pallas_call(put_out, out_shape=(jax.ShapeDtypeStruct((1, krylov + 1),...  0.63 us

profile of v2, /device:TPU:0, one launch (start us, length us, event | category | flops | bytes accessed | tf_op | source)
XLA Modules:
  0.0 16.7 jit_solution(12279383839277794644)
XLA Ops:
  0.6 15.4 %gmres_step.1 = (f32[1,21]{1,0:T(1,128)S(1)}, f32[64,128]{1,0:T(8,128)S(1)}) custom-call(f32[1280,128]{1,0:T(8,128)} %bitcast.4, bf16[64,128,128]{2,1,0:T(8,128)(2,1)} %precond_h.1, f32[32,128]{1,0:T(8,128)} %leaf_h.1, s32[1,32]{1,0:T(1,128)} %bitcast.5, f32[32,128]{1,0:T(8,128)} %strad_h.1, s32[1,32]{1,0:T(1,128)} %bitcast.6, s32[1,4]{1,0:T(1,128)} %count_h.1), custom_call_target="tpu_custom_call" | custom-call | tf_op jit(solution)/shard_map/gmres_step/pallas_call | solution.py:284
  16.1 0.6 %put_out.1 = (f32[1,21]{1,0:T(1,128)}, f32[64,128]{1,0:T(8,128)}) custom-call(f32[1,21]{1,0:T(1,128)S(1)} %get-tuple-element.6.coef_ref, f32[64,128]{1,0:T(8,128)S(1)} %get-tuple-element.7.next_ref), custom_call_target="tpu_custom_call" | custom-call | tf_op jit(solution)/shard_map/put_out/pallas_call | solution.py:322

commit v3 on v2

--- a/solution.py
+++ b/solution.py
@@ -38,7 +38,7 @@
     basis, precond, leaf, leaf_id, strad, strad_id, count,
     leaf_out, leaf_in, strad_out, strad_in,
     gram_out, gram_in, gram2_out, gram2_in, dots_out, dots_in,
-    field_ref, local_sem, sem,
+    field_ref, turned, local_sem, sem,
 ):
     g, m = lax.axis_index("grp"), lax.axis_index("mem")
     devices = groups * members
@@ -50,10 +50,10 @@
     barrier = pltpu.get_barrier_semaphore()
     mates = [lax.rem(m + o, members) for o in range(1, members)]
     peers = [lax.rem(g + o, groups) for o in range(1, groups)]
+    for peer in peers:
+        pl.semaphore_signal(barrier, inc=1, device_id=(peer, m), device_id_type=MESH)
     for mate in mates:
         pl.semaphore_signal(barrier, inc=1, device_id=(g, mate), device_id_type=MESH)
-    for peer in peers:
-        pl.semaphore_signal(barrier, inc=1, device_id=(peer, m), device_id_type=MESH)
 
     loads = [
         pltpu.make_async_copy(src, dst, local_sem.at[i])
@@ -152,6 +152,13 @@
     for mate in mates[::-1]:
         send(gram_out, gram_in.at[m], 4, (g, mate))
 
+    def turn(f, carry):
+        for j in range(4):
+            turned[4 * f + j] = precond[4 * f + j].T
+        return carry
+
+    lax.fori_loop(0, fibers // 4, turn, 0)
+
     wait_bytes(leaf_in.at[pl.ds(0, members - 1)], 1)
     wait_bytes(strad_in.at[pl.ds(0, groups - 1)], 3)
     leaf_got = leaf_in[...]
@@ -178,6 +185,7 @@
 
     block = 16
     pieces = []
+    sums = [jnp.zeros((8, width), jnp.float32)] * (krylov + 1)
     for t in range(fibers // block):
         tile = field_ref[t * block:(t + 1) * block, :]
         lhs = jnp.concatenate(
@@ -187,15 +195,16 @@
             ],
             axis=1,
         )
-        rhs = jnp.concatenate([precond[t * block + j] for j in range(block)], axis=1)
-        pieces.append(lax.dot_general(lhs, rhs, NT, preferred_element_type=jnp.float32))
+        rhs = jnp.concatenate([turned[t * block + j] for j in range(block)], axis=0)
+        piece = jnp.dot(lhs, rhs, preferred_element_type=jnp.float32)
+        pieces.append(piece)
+        for k in range(krylov + 1):
+            first = k * fibers + t * block
+            other = piece if k == krylov else basis[first:first + block, :]
+            product = (other * piece).reshape(block // 8, 8, width)
+            sums[k] = sums[k] + jnp.sum(product, axis=0)
     applied = jnp.concatenate(pieces, axis=0)
-
-    sums = []
-    for k in range(krylov + 1):
-        other = applied if k == krylov else basis[k * fibers:(k + 1) * fibers, :]
-        product = jnp.sum((other * applied).reshape(fibers // 8, 8, width), axis=0)
-        sums.append(jnp.sum(product, axis=0, keepdims=True))
+    sums = [jnp.sum(x, axis=0, keepdims=True) for x in sums]
     rows_of = pl.cdiv(krylov + 1, 8) * 8
     sums.append(jnp.zeros((rows_of - krylov - 1, width), jnp.float32))
     column = jnp.sum(jnp.concatenate(sums, axis=0), axis=1, keepdims=True)
@@ -206,7 +215,7 @@
     dots_out[...] = dots
     dots_in[me] = dots
     if devices <= 64:
-        for i in range(groups * members - 1, 0, -1):
+        for i in range(1, groups * members):
             to = (([g] + peers)[i // members], ([m] + mates)[i % members])
             send(dots_out, dots_in.at[me], 8, to)
     else:
@@ -310,6 +319,7 @@
             pltpu.VMEM((1, width), f32),
             pltpu.VMEM((devices, 1, width), f32),
             pltpu.VMEM((fibers, width), f32),
+            pltpu.VMEM(precond.shape, precond.dtype),
             pltpu.SemaphoreType.DMA((7,)),
             pltpu.SemaphoreType.DMA((10,)),
         ],

time: 17 us -> 16.6 us (0.976)
  Pallas kernels: 16.1 us -> 15.7 us
    pallas_call x1, Pallas kernels: 15.4 us -> 15.1 us  [local(): pl.pallas_call(functools.partial(kernel, groups, members, krylov, fibers,...]
where the time goes in v3:
time: 16.6 us; the launch traced here: 16.3 us
  Pallas kernels  15.7 us (95%)
  between operations  0.64 us (4%)
    pallas_call x1, Pallas kernels, local(): pl.pallas_call(functools.partial(kernel, groups, members, krylov, fibers,...  15.1 us
    pallas_call x1, Pallas kernels, local(): pl.pallas_call(put_out, out_shape=(jax.ShapeDtypeStruct((1, krylov + 1),...  0.63 us

profile of v3, /device:TPU:0, one launch (start us, length us, event | category | flops | bytes accessed | tf_op | source)
XLA Modules:
  0.0 16.3 jit_solution(4721452071790216948)
XLA Ops:
  0.6 15.1 %gmres_step.1 = (f32[1,21]{1,0:T(1,128)S(1)}, f32[64,128]{1,0:T(8,128)S(1)}) custom-call(f32[1280,128]{1,0:T(8,128)} %bitcast.4, bf16[64,128,128]{2,1,0:T(8,128)(2,1)} %precond_h.1, f32[32,128]{1,0:T(8,128)} %leaf_h.1, s32[1,32]{1,0:T(1,128)} %bitcast.5, f32[32,128]{1,0:T(8,128)} %strad_h.1, s32[1,32]{1,0:T(1,128)} %bitcast.6, s32[1,4]{1,0:T(1,128)} %count_h.1), custom_call_target="tpu_custom_call" | custom-call | tf_op jit(solution)/shard_map/gmres_step/pallas_call | solution.py:293
  15.7 0.6 %put_out.1 = (f32[1,21]{1,0:T(1,128)}, f32[64,128]{1,0:T(8,128)}) custom-call(f32[1,21]{1,0:T(1,128)S(1)} %get-tuple-element.6.coef_ref, f32[64,128]{1,0:T(8,128)S(1)} %get-tuple-element.7.next_ref), custom_call_target="tpu_custom_call" | custom-call | tf_op jit(solution)/shard_map/put_out/pallas_call | solution.py:332

commit v4 on v3

--- a/solution.py
+++ b/solution.py
@@ -61,7 +61,7 @@
             [
                 (leaf_h, leaf), (leaf_id_h, leaf_id), (strad_h, strad),
                 (count_h, count), (strad_id_h, strad_id),
-                (basis_h, basis), (precond_h, precond),
+                (basis_h, basis.at[pl.ds(0, krylov * fibers)]), (precond_h, precond),
             ]
         )
     ]
@@ -180,7 +180,7 @@
         + lax.dot_general(sel, mid, TN, preferred_element_type=jnp.float32)
         + lax.dot_general(sel, low, TN, preferred_element_type=jnp.float32)
     )
-    field = basis[(krylov - 1) * fibers:, :] + moved
+    field = basis[(krylov - 1) * fibers:krylov * fibers, :] + moved
     field_ref[...] = field.astype(jnp.bfloat16).astype(jnp.float32)
 
     block = 16
@@ -301,7 +301,7 @@
         in_specs=[any_space] * 7,
         out_specs=(vmem, vmem),
         scratch_shapes=[
-            pltpu.VMEM((krylov * fibers, width), f32),
+            pltpu.VMEM((tiles * 8 * fibers, width), f32),
             pltpu.VMEM(precond.shape, precond.dtype),
             pltpu.VMEM(leaf_rows.shape, f32),
             pltpu.VMEM((1, leaf_fiber.shape[0]), i32),

time: 16.6 us -> 16.6 us (level)
  no operation moved by 1% of the time
where the time goes in v4:
time: 16.6 us; the launch traced here: 16.3 us
  Pallas kernels  15.7 us (95%)
  between operations  0.64 us (4%)
    pallas_call x1, Pallas kernels, local(): pl.pallas_call(functools.partial(kernel, groups, members, krylov, fibers,...  15.1 us
    pallas_call x1, Pallas kernels, local(): pl.pallas_call(put_out, out_shape=(jax.ShapeDtypeStruct((1, krylov + 1),...  0.63 us

profile of v4, /device:TPU:0, one launch (start us, length us, event | category | flops | bytes accessed | tf_op | source)
XLA Modules:
  0.0 16.3 jit_solution(3898611361688631600)
XLA Ops:
  0.6 15.1 %gmres_step.1 = (f32[1,21]{1,0:T(1,128)S(1)}, f32[64,128]{1,0:T(8,128)S(1)}) custom-call(f32[1280,128]{1,0:T(8,128)} %bitcast.4, bf16[64,128,128]{2,1,0:T(8,128)(2,1)} %precond_h.1, f32[32,128]{1,0:T(8,128)} %leaf_h.1, s32[1,32]{1,0:T(1,128)} %bitcast.5, f32[32,128]{1,0:T(8,128)} %strad_h.1, s32[1,32]{1,0:T(1,128)} %bitcast.6, s32[1,4]{1,0:T(1,128)} %count_h.1), custom_call_target="tpu_custom_call" | custom-call | tf_op jit(solution)/shard_map/gmres_step/pallas_call | solution.py:293
  15.7 0.6 %put_out.1 = (f32[1,21]{1,0:T(1,128)}, f32[64,128]{1,0:T(8,128)}) custom-call(f32[1,21]{1,0:T(1,128)S(1)} %get-tuple-element.6.coef_ref, f32[64,128]{1,0:T(8,128)S(1)} %get-tuple-element.7.next_ref), custom_call_target="tpu_custom_call" | custom-call | tf_op jit(solution)/shard_map/put_out/pallas_call | solution.py:332
